TPU v7x, 512 devices: a whole 4x8x8 slice. The times are simulated.
512 devices in a mesh: rows: 16 (over x, y_lo, core), pairs: 32 (over y_hi, z).
Axes of the slice: x: 4, y: 8 (y_hi: 4, y_lo: 2; y = y_hi * 2 + y_lo), z: 8, core: 2. Of those that a mesh axis runs over, the one named last changes fastest.
Arguments:
- snapshots: float32 [32768, 8192], P('rows', 'pairs'), may hold values from -1600 to 1600, as said below
Outputs:
- rotated: float32 [32768, 8192], P('rows', 'pairs')
Inputs may be any that keep to these rules, and one draw needn't show every extreme that they name: `snapshots`: finite real values.
All inputs are finite; a program needn't handle non-finite values.
Results may differ from a plain program's by a relative error of at most 0.00011.
Values sent between devices are 32-bit elements; how exact they have to be, the bound alone decides.
A program may use at most 64 MiB of HBM per device.

v0:
```python
import jax
import jax.numpy as jnp
from jax import lax
from jax.sharding import PartitionSpec as P


def from_behind(value, axis, steps):
    count = lax.axis_size(axis)
    leading, last = (max(0, -steps), min(count, count - steps))
    return lax.ppermute(value, axis, [(source, source + steps) for source in range(leading, last)])


def gram_of(left, right):
    return lax.dot_general(left, right, (((0,), (0,)), ((), ())), precision=lax.Precision.HIGHEST)


def finish(pair, gram, total):
    scaled = gram / total
    identity = jnp.eye(gram.shape[0], dtype=pair.dtype)
    level = jnp.trace(scaled) / gram.shape[0]
    lower = jnp.linalg.cholesky(scaled + 0.1 * level * identity)
    inverse = lax.linalg.triangular_solve(lower, identity, left_side=True, lower=True)
    return jnp.dot(pair, inverse.T, precision=lax.Precision.HIGHEST)


def per_device(snapshots):
    local_rows = snapshots.shape[0]
    total = local_rows * lax.axis_size("rows")
    width = snapshots.shape[1] // 2
    count = lax.axis_size("pairs")
    index = lax.axis_index("pairs")
    first = index == 0
    last = index == count - 1
    pair = snapshots
    gram = lax.psum(gram_of(pair, pair), "rows")
    pair = finish(pair, gram, total)
    top = pair[:, :width]
    bottom = pair[:, width:]
    outgoing = jnp.where(first, bottom, top)
    arrived_top = from_behind(outgoing, "pairs", 1)
    arrived_bottom = from_behind(bottom, "pairs", -1)
    top_next = jnp.where(first, top, arrived_top)
    bottom_next = jnp.where(last, top, arrived_bottom)
    pair = jnp.concatenate([top_next, bottom_next], axis=1)
    gram = lax.psum(gram_of(pair, pair), "rows")
    pair = finish(pair, gram, total)
    return pair


def solution(mesh):
    return jax.shard_map(
        per_device,
        mesh=mesh,
        in_specs=(P("rows", "pairs"),),
        out_specs=P("rows", "pairs"),
        check_vma=False,
    )
```

profile of v0, /device:TPU:1, one launch (start us, length us, event | category | flops | bytes accessed | tf_op | source)
XLA Modules:
  0.0 497.8 jit_solution(18300253455600902669)
XLA Ops:
  6.5 1.6 copy-done
  8.1 4.2 fusion.30
  12.8 131.7 %all-reduce.4.cloned.1.call-done = f32[256,256]{0,1:T(8,128)} async-done(((f32[256,256]{0,1:T(8,128)}), f32[256,256]{0,1:T(8,128)}) %all-reduce.4.cloned.1.call-update) | async-done | bytes 262160 | tf_op jit(solution)/shard_map/psum | solution.py:35
  144.5 1.6 select_reduce_fusion.1
  146.7 1.0 select_add_fusion.1
  147.8 1.0 fusion.9
  148.9 11.7 %cholesky.130 = f32[128,128]{1,0:T(8,128)S(1)} custom-call(f32[128,128]{1,0:T(8,128)S(1)} %cholesky.194), custom_call_target="Cholesky" | custom-call | tf_op jit(solution)/shard_map/jit(cholesky)/cholesky | solution.py:21
  160.6 9.8 %custom-call.13 = f32[1,128,128]{1,2,0:T(8,128)S(1)} custom-call(f32[1,128,128]{2,1,0:T(8,128)S(1)} %get-tuple-element.54), custom_call_target="InvertDiagBlocksLowerTriangular" | custom-call | tf_op jit(solution)/shard_map/jit(cholesky)/cholesky | solution.py:21
  170.9 11.7 %cholesky.147 = f32[128,128]{1,0:T(8,128)S(1)} custom-call(f32[128,128]{1,0:T(8,128)S(1)} %convolution_subtract_fusion.3), custom_call_target="Cholesky" | custom-call | tf_op jit(solution)/shard_map/jit(cholesky)/cholesky | solution.py:21
  182.7 0.7 compare_reduce_fusion.2
  184.9 16.2 %while.4 = (s32[]{:T(128)}, f32[256,256]{1,0:T(8,128)S(1)}, s32[2,2]{1,0:T(2,128)S(1)}, f32[2,128,128]{2,1,0:T(8,128)S(1)}, s32[]{:T(128)}) while((s32[]{:T(128)}, f32[256,256]{1,0:T(8,128)S(1)}, s32[2,2]{1,0:T(2,128)S(1)}, f32[2,128,128]{2,1,0:T(8,128)S(1)}, s32[]{:T(128)}) %tuple.45), condition=%wide.while_cond, body=%wide.while_body.sunk | while | flops 2 | bytes 131181 | solution.py:22
  197.6 1.4 bitcast_dynamic-update-slice_fusion.4
  199.6 1.4 bitcast_dynamic-update-slice_fusion.4
  201.1 19.7 %custom-call.14 = f32[2,128,128]{1,2,0:T(8,128)S(1)} custom-call(f32[2,128,128]{2,1,0:T(8,128)S(1)} %get-tuple-element.21), custom_call_target="InvertDiagBlocksLowerTriangular" | custom-call | tf_op jit(solution)/shard_map/triangular_solve/custom-call.0 | solution.py:22
  221.8 1.9 convolution_bitcast_fusion
  223.8 1.4 slice_select_fusion.2
  225.4 4.3 collective-permute-start
  229.7 1.3 collective-permute-start.1
  231.0 19.8 %collective-permute-done = f32[2048,128]{0,1:T(8,128)} collective-permute-done((f32[2048,128]{0,1:T(8,128)}, f32[2048,128]{0,1:T(8,128)}, u32[]{:S(2)}, u32[]{:S(2)}) %collective-permute-start) | collective-permute-done | bytes 1048608 | tf_op jit(solution)/shard_map/ppermute | solution.py:10
  250.8 4.6 collective-permute-done.1
  255.4 1.7 slice_select_fusion.1
  257.2 1.0 copy-done.2
  258.2 2.6 fusion.1
  260.8 145.7 %all-reduce.6.cloned.1.call-done = f32[256,256]{0,1:T(8,128)} async-done(((f32[256,256]{0,1:T(8,128)}), f32[256,256]{0,1:T(8,128)}) %all-reduce.6.cloned.1.call-update) | async-done | bytes 262160 | tf_op jit(solution)/shard_map/psum | solution.py:45
  406.4 1.6 select_reduce_fusion
  408.7 1.7 select_add_fusion
  410.4 1.8 copy.5
  412.2 1.1 fusion.8
  413.3 0.7 copy-done.3
  414.0 11.7 %cholesky.164 = f32[128,128]{1,0:T(8,128)S(1)} custom-call(f32[128,128]{1,0:T(8,128)S(1)} %cholesky.197), custom_call_target="Cholesky" | custom-call | tf_op jit(solution)/shard_map/jit(cholesky)/cholesky | solution.py:21
  425.7 0.7 cholesky.189
  426.4 9.8 %custom-call.15 = f32[1,128,128]{1,2,0:T(8,128)S(1)} custom-call(f32[1,128,128]{2,1,0:T(8,128)S(1)} %get-tuple-element.50), custom_call_target="InvertDiagBlocksLowerTriangular" | custom-call | tf_op jit(solution)/shard_map/jit(cholesky)/cholesky | solution.py:21
  436.3 1.7 constant_dynamic-update-slice_fusion.1
  437.9 1.1 convolution_subtract_fusion.2
  439.0 11.9 %cholesky.181 = f32[128,128]{1,0:T(8,128)S(1)} custom-call(f32[128,128]{1,0:T(8,128)S(1)} %convolution_subtract_fusion.2), custom_call_target="Cholesky" | custom-call | tf_op jit(solution)/shard_map/jit(cholesky)/cholesky | solution.py:21
  450.9 0.6 select_reduce_fusion.2
  451.6 0.6 compare_reduce_fusion
  452.2 0.7 compare_reduce_fusion.1
  454.2 1.7 select_select_fusion
  455.9 5.8 %while.5 = (s32[]{:T(128)}, f32[256,256]{1,0:T(8,128)}, s32[2,2]{1,0:T(2,128)S(1)}, f32[2,128,128]{2,1,0:T(8,128)S(1)}, s32[]{:T(128)}) while((s32[]{:T(128)}, f32[256,256]{1,0:T(8,128)}, s32[2,2]{1,0:T(2,128)S(1)}, f32[2,128,128]{2,1,0:T(8,128)S(1)}, s32[]{:T(128)}) %tuple.55), condition=%wide.while_cond.clone, body=%wide.while_body.clone.sunk | while | flops 2 | bytes 131181 | solution.py:22
  455.9 0.7 fusion.45
  456.5 2.3 bitcast_dynamic-update-slice_fusion.5
  458.8 0.7 fusion.45
  459.5 2.2 bitcast_dynamic-update-slice_fusion.5
  461.7 0.6 copy-done.4
  462.3 20.5 %custom-call.16 = f32[2,128,128]{1,2,0:T(8,128)S(1)} custom-call(f32[2,128,128]{2,1,0:T(8,128)} %copy-done.4), custom_call_target="InvertDiagBlocksLowerTriangular" | custom-call | tf_op jit(solution)/shard_map/triangular_solve/custom-call.0 | solution.py:22
  483.1 1.2 convolution_subtract_fusion
  484.7 6.0 %fusion = f32[2048,256]{1,0:T(8,128)} fusion(f32[2048,128]{0,1:T(8,128)} %copy-done.2, f32[2048,128]{0,1:T(8,128)S(1)} %get-tuple-element.43, f32[128,256]{1,0:T(8,128)S(1)} %fusion.16, f32[128,256]{1,0:T(8,128)S(1)} %fusion.11), kind=kOutput, calls=%fused_computation.6 | convolution fusion | flops 1611202560 | bytes 4456448 | tf_op jit(solution)/shard_map/dot_general | solution.py:23
  (36 shorter events, 4.5 us)
Async XLA Ops:
  6.5 1.6 copy-start
  6.5 137.9 %all-reduce.4.cloned.1.call-start = ((), (), s32[]{:S(2)}) async-start(), calls=%async_computation | async-start | bytes 524288 | tf_op jit(solution)/shard_map/psum | solution.py:35
  12.3 394.1 %all-reduce.6.cloned.1.call-start = ((), (), s32[]{:S(2)}) async-start(), calls=%async_computation.1 | async-start | bytes 524288 | tf_op jit(solution)/shard_map/psum | solution.py:45
  223.8 1.7 copy-start.1
  225.4 25.4 %collective-permute-start = (f32[2048,128]{0,1:T(8,128)}, f32[2048,128]{0,1:T(8,128)}, u32[]{:S(2)}, u32[]{:S(2)}) collective-permute-start(f32[2048,128]{0,1:T(8,128)} %get-tuple-element.45), channel_id=1, source_target_pairs={{0,1},{1,2},{2,3},{3,4},{4,5},{5,6},{6,7},{7,8},{8,9},{9,10},{10,1... | collective-permute-start | bytes 3145736 | tf_op jit(solution)/shard_map/ppermute | solution.py:10
  229.7 25.7 %collective-permute-start.1 = (f32[2048,128]{0,1:T(8,128)S(1)}, f32[2048,128]{0,1:T(8,128)}, u32[]{:S(2)}, u32[]{:S(2)}) collective-permute-start(f32[2048,128]{0,1:T(8,128)S(1)} %get-tuple-element.46), channel_id=1, source_target_pairs={{1,0},{2,1},{3,2},{4,3},{5,4},{6,5},{7,6},{8,7},{9,8},{10,9},{11,1... | collective-permute-start | bytes 3145736 | tf_op jit(solution)/shard_map/ppermute | solution.py:10
  257.2 1.0 copy-start.2
  413.2 0.7 copy-start.3
  461.7 0.6 copy-start.4
Sparse Core Ops, SparseCore 0:
  12.4 132.0 all-reduce.3
  260.9 145.5 all-reduce.5
where the time goes:
time: 502 us; the launch traced here: 498 us
  waiting for transfers between devices  302 us (60%)
  other arithmetic  122 us (24%)
  matrix products  20.8 us (4%)
  between operations  17.8 us (4%)
  local copies, waits for them, and re-layouts  16.8 us (3%)
  loops' own time  12.2 us (2%)
  starting transfers between devices  6 us (1%)
    psum x2, waiting for transfers between devices, per_device(): gram = lax.psum(gram_of(pair, pair), 'rows')  277 us
    another operation x13, other arithmetic, finish(): lower = jnp.linalg.cholesky(scaled + 0.1 * level * identity)  69.5 us
    another operation x5, other arithmetic, finish(): lax.linalg.triangular_solve(lower, identity, left_side=True, lower=True)  41.9 us
    ppermute x2, waiting for transfers between devices, from_behind(): lax.ppermute(value, axis, [(source, source + steps) for source in range(l...  24.4 us
    another operation x2, loops' own time, finish(): lax.linalg.triangular_solve(lower, identity, left_side=True, lower=True)  12.2 us
  transfers between devices with their start and end apart: 4, of which 4 were waited for; matrix products, arithmetic and copies ran while one was open for 0% of the time, Pallas kernels for 0%

commit v1 on v0

--- a/solution.py
+++ b/solution.py
@@ -32,7 +32,8 @@
     first = index == 0
     last = index == count - 1
     pair = snapshots
-    gram = lax.psum(gram_of(pair, pair), "rows")
+    values_pass = lambda panel, ax_name: jnp.sum(lax.all_gather(panel, ax_name), 0)
+    gram = values_pass(gram_of(pair, pair), "rows")
     pair = finish(pair, gram, total)
     top = pair[:, :width]
     bottom = pair[:, width:]

time: 502 us -> 422 us (0.84)
  waiting for transfers between devices: 302 us -> 222 us
    psum x2 -> x1, waiting for transfers between devices: 277 us -> 149 us  [per_device(): gram = lax.psum(gram_of(pair, pair), 'rows')]
    all_gather x0 -> x1, waiting for transfers between devices: none -> 48.2 us  [per_device(): lax.all_gather(panel, ax_name)]
where the time goes in v1:
time: 422 us; the launch traced here: 418 us
  waiting for transfers between devices  222 us (53%)
  other arithmetic  122 us (29%)
  matrix products  20.8 us (5%)
  between operations  17.8 us (4%)
  local copies, waits for them, and re-layouts  17 us (4%)
  loops' own time  12.2 us (3%)
  starting transfers between devices  6 us (1%)
    psum x1, waiting for transfers between devices, per_device(): gram = lax.psum(gram_of(pair, pair), 'rows')  149 us
    another operation x13, other arithmetic, finish(): lower = jnp.linalg.cholesky(scaled + 0.1 * level * identity)  69.5 us
    all_gather x1, waiting for transfers between devices, per_device(): lax.all_gather(panel, ax_name)  48.2 us
    another operation x5, other arithmetic, finish(): lax.linalg.triangular_solve(lower, identity, left_side=True, lower=True)  41.9 us
    ppermute x2, waiting for transfers between devices, from_behind(): lax.ppermute(value, axis, [(source, source + steps) for source in range(l...  24.9 us
    another operation x2, loops' own time, finish(): lax.linalg.triangular_solve(lower, identity, left_side=True, lower=True)  12.2 us
    another operation x15, local copies, waits for them, and re-layouts, finish(): lax.linalg.triangular_solve(lower, identity, left_side=True, lower=True)  9.92 us
  transfers between devices with their start and end apart: 4, of which 4 were waited for; matrix products, arithmetic and copies ran while one was open for 0% of the time, Pallas kernels for 0%

profile of v1, /device:TPU:1, one launch (start us, length us, event | category | flops | bytes accessed | tf_op | source)
XLA Modules:
  0.0 417.6 jit_solution(9291367935673095638)
XLA Ops:
  6.5 1.6 copy-done
  8.1 4.2 %fusion.30 = f32[256,256]{1,0:T(8,128)} fusion(f32[2048,256]{1,0:T(8,128)S(1)} %copy-done), kind=kOutput, calls=%fused_computation.74 | convolution fusion | flops 1610612736 | bytes 2359296 | tf_op jit(solution)/shard_map/dot_general | solution.py:14
  12.8 48.2 %all-gather.3.cloned.1.call-done = f32[4096,256]{1,0:T(8,128)} async-done(((f32[256,256]{1,0:T(8,128)}), f32[4096,256]{1,0:T(8,128)}) %all-gather.3.cloned.1.call-update) | async-done | bytes 4194320 | tf_op jit(solution)/shard_map/all_gather | solution.py:35
  61.1 2.5 reduce_sum.25
  63.7 0.6 select_reduce_fusion.1
  65.2 11.7 %cholesky.130 = f32[128,128]{1,0:T(8,128)S(1)} custom-call(f32[128,128]{1,0:T(8,128)S(1)} %cholesky.194), custom_call_target="Cholesky" | custom-call | tf_op jit(solution)/shard_map/jit(cholesky)/cholesky | solution.py:21
  77.0 9.8 %custom-call.13 = f32[1,128,128]{1,2,0:T(8,128)S(1)} custom-call(f32[1,128,128]{2,1,0:T(8,128)S(1)} %get-tuple-element.54), custom_call_target="InvertDiagBlocksLowerTriangular" | custom-call | tf_op jit(solution)/shard_map/jit(cholesky)/cholesky | solution.py:21
  87.3 11.7 %cholesky.147 = f32[128,128]{1,0:T(8,128)S(1)} custom-call(f32[128,128]{1,0:T(8,128)S(1)} %convolution_subtract_fusion.3), custom_call_target="Cholesky" | custom-call | tf_op jit(solution)/shard_map/jit(cholesky)/cholesky | solution.py:21
  99.0 0.7 compare_reduce_fusion.2
  101.2 16.2 %while.4 = (s32[]{:T(128)}, f32[256,256]{1,0:T(8,128)S(1)}, s32[2,2]{1,0:T(2,128)S(1)}, f32[2,128,128]{2,1,0:T(8,128)S(1)}, s32[]{:T(128)}) while((s32[]{:T(128)}, f32[256,256]{1,0:T(8,128)S(1)}, s32[2,2]{1,0:T(2,128)S(1)}, f32[2,128,128]{2,1,0:T(8,128)S(1)}, s32[]{:T(128)}) %tuple.45), condition=%wide.while_cond, body=%wide.while_body.sunk | while | flops 2 | bytes 131181 | solution.py:22
  113.3 0.6 fusion.44
  113.9 1.4 bitcast_dynamic-update-slice_fusion.4
  116.0 1.4 bitcast_dynamic-update-slice_fusion.4
  117.4 19.7 %custom-call.14 = f32[2,128,128]{1,2,0:T(8,128)S(1)} custom-call(f32[2,128,128]{2,1,0:T(8,128)S(1)} %get-tuple-element.21), custom_call_target="InvertDiagBlocksLowerTriangular" | custom-call | tf_op jit(solution)/shard_map/triangular_solve/custom-call.0 | solution.py:22
  138.1 1.9 convolution_bitcast_fusion
  140.1 1.4 slice_select_fusion.2
  141.8 4.3 %collective-permute-start = (f32[2048,128]{0,1:T(8,128)}, f32[2048,128]{0,1:T(8,128)}, u32[]{:S(2)}, u32[]{:S(2)}) collective-permute-start(f32[2048,128]{0,1:T(8,128)} %get-tuple-element.45), channel_id=1, source_target_pairs={{0,1},{1,2},{2,3},{3,4},{4,5},{5,6},{6,7},{7,8},{8,9},{9,10},{10,1... | collective-permute-start | bytes 3145736 | tf_op jit(solution)/shard_map/ppermute | solution.py:10
  146.1 1.3 collective-permute-start.1
  147.4 20.3 %collective-permute-done = f32[2048,128]{0,1:T(8,128)} collective-permute-done((f32[2048,128]{0,1:T(8,128)}, f32[2048,128]{0,1:T(8,128)}, u32[]{:S(2)}, u32[]{:S(2)}) %collective-permute-start) | collective-permute-done | bytes 1048608 | tf_op jit(solution)/shard_map/ppermute | solution.py:10
  167.6 4.6 %collective-permute-done.1 = f32[2048,128]{0,1:T(8,128)} collective-permute-done((f32[2048,128]{0,1:T(8,128)S(1)}, f32[2048,128]{0,1:T(8,128)}, u32[]{:S(2)}, u32[]{:S(2)}) %collective-permute-start.1) | collective-permute-done | bytes 1048608 | tf_op jit(solution)/shard_map/ppermute | solution.py:10
  172.2 1.7 slice_select_fusion.1
  174.0 1.0 copy-done.2
  174.9 2.6 fusion.1
  177.5 148.7 %all-reduce.3.cloned.1.call-done = f32[256,256]{0,1:T(8,128)} async-done(((f32[256,256]{0,1:T(8,128)}), f32[256,256]{0,1:T(8,128)}) %all-reduce.3.cloned.1.call-update) | async-done | bytes 262160 | tf_op jit(solution)/shard_map/psum | solution.py:46
  326.3 1.6 select_reduce_fusion
  328.5 1.7 select_add_fusion
  330.2 1.8 copy.8
  332.0 1.1 fusion.8
  333.1 0.7 copy-done.3
  333.8 11.7 %cholesky.164 = f32[128,128]{1,0:T(8,128)S(1)} custom-call(f32[128,128]{1,0:T(8,128)S(1)} %cholesky.197), custom_call_target="Cholesky" | custom-call | tf_op jit(solution)/shard_map/jit(cholesky)/cholesky | solution.py:21
  345.5 0.7 cholesky.189
  346.3 9.8 %custom-call.15 = f32[1,128,128]{1,2,0:T(8,128)S(1)} custom-call(f32[1,128,128]{2,1,0:T(8,128)S(1)} %get-tuple-element.50), custom_call_target="InvertDiagBlocksLowerTriangular" | custom-call | tf_op jit(solution)/shard_map/jit(cholesky)/cholesky | solution.py:21
  356.1 1.7 constant_dynamic-update-slice_fusion.1
  357.8 1.1 convolution_subtract_fusion.2
  358.9 11.9 %cholesky.181 = f32[128,128]{1,0:T(8,128)S(1)} custom-call(f32[128,128]{1,0:T(8,128)S(1)} %convolution_subtract_fusion.2), custom_call_target="Cholesky" | custom-call | tf_op jit(solution)/shard_map/jit(cholesky)/cholesky | solution.py:21
  370.7 0.6 select_reduce_fusion.2
  371.4 0.6 compare_reduce_fusion
  372.0 0.7 compare_reduce_fusion.1
  374.0 1.7 select_select_fusion
  375.7 5.8 %while.5 = (s32[]{:T(128)}, f32[256,256]{1,0:T(8,128)}, s32[2,2]{1,0:T(2,128)S(1)}, f32[2,128,128]{2,1,0:T(8,128)S(1)}, s32[]{:T(128)}) while((s32[]{:T(128)}, f32[256,256]{1,0:T(8,128)}, s32[2,2]{1,0:T(2,128)S(1)}, f32[2,128,128]{2,1,0:T(8,128)S(1)}, s32[]{:T(128)}) %tuple.55), condition=%wide.while_cond.clone, body=%wide.while_body.clone.sunk | while | flops 2 | bytes 131181 | solution.py:22
  375.7 0.7 fusion.45
  376.4 2.3 bitcast_dynamic-update-slice_fusion.5
  378.7 0.7 fusion.45
  379.3 2.2 bitcast_dynamic-update-slice_fusion.5
  381.5 0.6 copy-done.4
  382.2 20.5 %custom-call.16 = f32[2,128,128]{1,2,0:T(8,128)S(1)} custom-call(f32[2,128,128]{2,1,0:T(8,128)} %copy-done.4), custom_call_target="InvertDiagBlocksLowerTriangular" | custom-call | tf_op jit(solution)/shard_map/triangular_solve/custom-call.0 | solution.py:22
  403.0 1.2 convolution_subtract_fusion
  404.5 6.0 %fusion = f32[2048,256]{1,0:T(8,128)} fusion(f32[2048,128]{0,1:T(8,128)} %copy-done.2, f32[2048,128]{0,1:T(8,128)S(1)} %get-tuple-element.43, f32[128,256]{1,0:T(8,128)S(1)} %fusion.16, f32[128,256]{1,0:T(8,128)S(1)} %fusion.11), kind=kOutput, calls=%fused_computation.6 | convolution fusion | flops 1611202560 | bytes 4456448 | tf_op jit(solution)/shard_map/dot_general | solution.py:23
  (38 shorter events, 4.1 us)
Async XLA Ops:
  6.5 1.6 copy-start
  6.5 54.5 %all-gather.3.cloned.1.call-start = ((), (), s32[]{:S(2)}) async-start(), calls=%async_computation.1 | async-start | bytes 4456448 | tf_op jit(solution)/shard_map/all_gather | solution.py:35
  12.3 313.9 %all-reduce.3.cloned.1.call-start = ((), (), s32[]{:S(2)}) async-start(), calls=%async_computation | async-start | bytes 524288 | tf_op jit(solution)/shard_map/psum | solution.py:46
  140.1 1.7 copy-start.1
  141.8 25.8 %collective-permute-start = (f32[2048,128]{0,1:T(8,128)}, f32[2048,128]{0,1:T(8,128)}, u32[]{:S(2)}, u32[]{:S(2)}) collective-permute-start(f32[2048,128]{0,1:T(8,128)} %get-tuple-element.45), channel_id=1, source_target_pairs={{0,1},{1,2},{2,3},{3,4},{4,5},{5,6},{6,7},{7,8},{8,9},{9,10},{10,1... | collective-permute-start | bytes 3145736 | tf_op jit(solution)/shard_map/ppermute | solution.py:10
  146.1 26.2 %collective-permute-start.1 = (f32[2048,128]{0,1:T(8,128)S(1)}, f32[2048,128]{0,1:T(8,128)}, u32[]{:S(2)}, u32[]{:S(2)}) collective-permute-start(f32[2048,128]{0,1:T(8,128)S(1)} %get-tuple-element.46), channel_id=1, source_target_pairs={{1,0},{2,1},{3,2},{4,3},{5,4},{6,5},{7,6},{8,7},{9,8},{10,9},{11,1... | collective-permute-start | bytes 3145736 | tf_op jit(solution)/shard_map/ppermute | solution.py:10
  174.0 1.0 copy-start.2
  333.1 0.7 copy-start.3
  381.5 0.6 copy-start.4
Sparse Core Ops, SparseCore 0:
  12.5 48.5 all-gather.2
  177.7 148.5 all-reduce.2
